TPU v7x, 32 devices: a whole 2x2x4 slice. The times are simulated.
32 devices in a mesh: seq: 8 (over z, y), tp: 4 (over x, core).
Axes of the slice: x: 2, y: 2, z: 4, core: 2. Of those that a mesh axis runs over, the one named last changes fastest.
Arguments:
- tokens: bfloat16 [2048, 2560], P('seq', 'tp'), may hold values from -6 to 6
- segments: int32 [8, 256], P('seq'), may hold values from 0 to 3, never falling along the last dimension, each value on 1 to 128 neighbouring positions
- routes: int32 [2048, 6], P('seq'), may hold values from 0 to 63, all different within a row; in each aligned block of 256 rows (0 to 255, 256 to 511, ...) at most 40 rows name the same one
- page_table: int32 [8, 32], P('seq'), may hold values from 0 to 31, each once within a row
- cache_pool: bfloat16 [256, 16, 1024], P('seq', None, 'tp'), may hold values from -6 to 6
- attn_gain: float32 [2560], replicated, may hold values from 0.1 to 1.9
- w_query: bfloat16 [2560, 2048], P(None, 'tp'), may hold values from -0.125 to 0.125
- w_keyval: bfloat16 [2560, 1024], P(None, 'tp'), may hold values from -0.125 to 0.125
- w_out: bfloat16 [2048, 2560], P('tp'), may hold values from -0.125 to 0.125
- ffn_gain: float32 [2560], replicated, may hold values from 0.1 to 1.9
- w_router: bfloat16 [2560, 64], replicated, may hold values from -0.125 to 0.125
- expert_gate: bfloat16 [64, 1536, 2560], P('seq', 'tp'), may hold values from -0.125 to 0.125
- expert_up: bfloat16 [64, 1536, 2560], P('seq', 'tp'), may hold values from -0.125 to 0.125
- expert_down: bfloat16 [64, 1536, 2560], P('seq', 'tp'), may hold values from -0.15625 to 0.15625
- shared_gate: bfloat16 [1536, 2560], P('tp'), may hold values from -0.125 to 0.125
- shared_up: bfloat16 [1536, 2560], P('tp'), may hold values from -0.125 to 0.125
- shared_down: bfloat16 [1536, 2560], P('tp'), may hold values from -0.15625 to 0.15625
Outputs:
- layer_out: bfloat16 [2048, 2560], P('seq', 'tp')
- cache_out: bfloat16 [256, 16, 1024], P('seq', None, 'tp')
Inputs may be any that keep to these rules, and one draw needn't show every extreme that they name: `segments`: each row is one worker's block; ids never fall along a row, every segment has 1 to 128 slots and one has exactly 128. `routes`: within the 256 tokens of one worker no expert is named more than 40 times, a bound that some block reaches. `page_table`: each row lists every page of one worker's pool once; its first 16 entries take the worker's blocks in order.
All inputs are finite; a program needn't handle non-finite values.
Results may differ from a plain program's by a relative error of at most 0.019.
Values may be sent and summed in bfloat16 or wider, within the bound.
A program may use at most 192 MiB of HBM per device.

v0:
```python
import jax
import jax.numpy as jnp
from jax import lax
from jax.sharding import PartitionSpec as P

HEAD = 128
PAGE = 16
norm_eps = 1e-05
rope_base = 500000.0


def partner(block, axis, distance):
    count = lax.axis_size(axis)
    route = []
    for low in range(count):
        high = low | 1 << distance
        if high != low and high < count:
            route += [(low, high), (high, low)]
    return lax.ppermute(block, axis, route)


def gather_all(block):
    return lax.all_gather(block, ("seq", "tp"), axis=0)


def scatter_all(whole):
    part = lax.psum_scatter(whole, "tp", scatter_dimension=2, tiled=True)
    return lax.psum_scatter(part, "seq", scatter_dimension=0, tiled=False)


def rms_scale(inputs, gain_vec):
    return (
        inputs * lax.rsqrt(jnp.mean(inputs * inputs, axis=-1, keepdims=True) + norm_eps) * gain_vec
    )


def in_segment(segment_row):
    row_order = jnp.arange(segment_row.shape[0], dtype=jnp.int32)
    before = (segment_row[:, None] == segment_row[None, :]) & (
        row_order[None, :] < row_order[:, None]
    )
    return jnp.sum(before.astype(jnp.int32), axis=1)


def rotate(inputs, position):
    half_size = inputs.shape[-1] // 2
    inv_freq = rope_base ** (-jnp.arange(half_size, dtype=jnp.float32) * 2.0 / inputs.shape[-1])
    angles = position.astype(jnp.float32)[:, None] * inv_freq[None, :]
    cosine = jnp.cos(angles)[:, None, :]
    sine_term = jnp.sin(angles)[:, None, :]
    leading = inputs[..., :half_size]
    trailing = inputs[..., half_size:]
    return jnp.concatenate(
        [leading * cosine - trailing * sine_term, trailing * cosine + leading * sine_term], axis=-1
    )


def shards(
    tokens,
    segments,
    routes,
    page_table,
    cache_pool,
    attn_gain,
    w_query,
    w_keyval,
    w_out,
    ffn_gain,
    w_router,
    expert_gate,
    expert_up,
    expert_down,
    shared_gate,
    shared_up,
    shared_down,
):
    tp_count = lax.axis_size("tp")
    seq_count = lax.axis_size("seq")
    tp_rank = lax.axis_index("tp")
    row_count = tokens.shape[0]
    col_width = tokens.shape[1]
    model_width = col_width * tp_count
    whole_rows = lax.all_gather(tokens, "tp", axis=1, tiled=True)
    residual = whole_rows.astype(jnp.float32)
    normed_in = rms_scale(residual, attn_gain).astype(jnp.bfloat16)
    segment_row = segments[0]
    position = in_segment(segment_row)
    local_heads = w_query.shape[1] // HEAD
    queries = jnp.dot(normed_in, w_query, preferred_element_type=jnp.float32).reshape(
        row_count, local_heads, HEAD
    )
    queries = rotate(queries, position).astype(jnp.bfloat16)
    keyval = jnp.dot(normed_in, w_keyval, preferred_element_type=jnp.float32)
    if w_keyval.shape[1] == HEAD:
        is_key = tp_rank % 2 == 0
        rotated = rotate(keyval.reshape(row_count, 1, HEAD), position).reshape(row_count, HEAD)
        own_half = jnp.where(is_key, rotated, keyval).astype(jnp.bfloat16)
        other_half = partner(own_half, "tp", 0)
        key_rows = jnp.where(is_key, own_half, other_half)
        values = jnp.where(is_key, other_half, own_half)
        cache_rows = own_half
    else:
        key_rows = (
            rotate(keyval[:, :HEAD].reshape(row_count, 1, HEAD), position)
            .reshape(row_count, HEAD)
            .astype(jnp.bfloat16)
        )
        values = keyval[:, HEAD:].astype(jnp.bfloat16)
        cache_rows = jnp.concatenate([key_rows, values], axis=1)
    scores = jnp.einsum(
        "qhd,kd->hqk", queries, key_rows, preferred_element_type=jnp.float32
    ) * HEAD ** (-0.5)
    row_order = jnp.arange(row_count, dtype=jnp.int32)
    allowed = (segment_row[:, None] == segment_row[None, :]) & (
        row_order[None, :] <= row_order[:, None]
    )
    weights = jnp.where(allowed[None], jnp.exp(scores), 0.0)
    attn_probs = (weights / jnp.sum(weights, axis=-1, keepdims=True)).astype(jnp.bfloat16)
    attended = jnp.einsum("hqk,kd->qhd", attn_probs, values, preferred_element_type=jnp.float32)
    attended = attended.astype(jnp.bfloat16).reshape(row_count, local_heads * HEAD)
    attn_part = jnp.dot(attended, w_out, preferred_element_type=jnp.float32)
    attn_mine = lax.psum_scatter(
        attn_part.astype(jnp.bfloat16), "tp", scatter_dimension=1, tiled=True
    )
    hidden_mine = tokens.astype(jnp.float32) + attn_mine.astype(jnp.float32)
    seq_rank = lax.axis_index("seq")
    gathered = gather_all(hidden_mine.astype(jnp.bfloat16))
    hidden_all = (
        gathered.reshape(seq_count, tp_count, row_count, col_width)
        .transpose(0, 2, 1, 3)
        .reshape(seq_count, row_count, model_width)
    )
    normed_all = rms_scale(hidden_all.astype(jnp.float32), ffn_gain).astype(jnp.bfloat16)
    top_count = routes.shape[1]
    local_experts = expert_gate.shape[0]
    expert_total = local_experts * seq_count
    capacity = (
        (row_count * top_count * 5 // (expert_total * 3) + tp_count - 1) // tp_count * tp_count
    )
    slots = local_experts * capacity
    routes_all = lax.all_gather(routes, "seq", axis=0)
    chosen = jnp.sum(
        (routes_all[:, :, :, None] == jnp.arange(expert_total, dtype=jnp.int32)).astype(
            jnp.float32
        ),
        axis=2,
    )
    logits = jnp.einsum("wtd,de->wte", normed_all, w_router, preferred_element_type=jnp.float32)
    lifted = jnp.where(chosen > 0, jnp.exp(logits), 0.0)
    route_weight = lifted / jnp.sum(lifted, axis=2, keepdims=True)
    first = seq_rank * local_experts
    named = lax.dynamic_slice_in_dim(chosen, first, local_experts, 2)
    weight_mine = lax.dynamic_slice_in_dim(route_weight, first, local_experts, 2)
    earlier = (row_order[:, None] > row_order[None, :]).astype(jnp.bfloat16)
    rank = jnp.einsum(
        "ts,wse->wte", earlier, named.astype(jnp.bfloat16), preferred_element_type=jnp.float32
    ).astype(jnp.int32)
    place = jnp.where(named > 0, rank, -1)
    hit = (
        place.transpose(0, 2, 1)[:, :, None, :]
        == jnp.arange(capacity, dtype=jnp.int32)[None, None, :, None]
    )
    select = hit.astype(jnp.bfloat16).reshape(seq_count, slots, row_count)
    slot_weight = jnp.sum(
        jnp.where(hit, weight_mine.transpose(0, 2, 1)[:, :, None, :], 0.0), axis=3
    )
    slot_rows = (
        jnp.einsum("wst,wtd->wsd", select, normed_all, preferred_element_type=jnp.float32)
        .astype(jnp.bfloat16)
        .reshape(seq_count, local_experts, capacity, model_width)
    )
    gate_out = jnp.einsum(
        "secd,efd->secf", slot_rows, expert_gate, preferred_element_type=jnp.float32
    )
    up_out = jnp.einsum("secd,efd->secf", slot_rows, expert_up, preferred_element_type=jnp.float32)
    activation = (jax.nn.silu(gate_out) * up_out * slot_weight[..., None]).astype(jnp.bfloat16)
    group_part = (
        jnp.einsum("secf,efd->secd", activation, expert_down, preferred_element_type=jnp.float32)
        .astype(jnp.bfloat16)
        .reshape(seq_count, slots, model_width)
    )
    normed_mid = lax.dynamic_index_in_dim(normed_all, seq_rank, 0, keepdims=False)
    shared_gate_out = jnp.einsum(
        "td,fd->tf", normed_mid, shared_gate, preferred_element_type=jnp.float32
    )
    shared_up_out = jnp.einsum(
        "td,fd->tf", normed_mid, shared_up, preferred_element_type=jnp.float32
    )
    shared_act = (jax.nn.silu(shared_gate_out) * shared_up_out).astype(jnp.bfloat16)
    shared_part = jnp.dot(shared_act, shared_down, preferred_element_type=jnp.float32)
    routed_part = jnp.einsum("wst,wsd->wtd", select, group_part, preferred_element_type=jnp.float32)
    is_mine = jnp.arange(seq_count, dtype=jnp.int32)[:, None, None] == seq_rank
    summand = routed_part + jnp.where(is_mine, shared_part[None], 0.0)
    output_share = scatter_all(summand.astype(jnp.bfloat16)).astype(jnp.float32)
    layer_out = (hidden_mine + output_share).astype(jnp.bfloat16)
    page_count = row_count // PAGE
    new_pages = cache_rows.reshape(page_count, PAGE, cache_rows.shape[1])
    cache_out = cache_pool.at[page_table[0, :page_count]].set(new_pages)
    return (layer_out, cache_out)


def solution(mesh):
    in_specs = (
        P("seq", "tp"),
        P("seq", None),
        P("seq", None),
        P("seq", None),
        P("seq", None, "tp"),
        P(),
        P(None, "tp"),
        P(None, "tp"),
        P("tp", None),
        P(),
        P(),
        P("seq", "tp", None),
        P("seq", "tp", None),
        P("seq", "tp", None),
        P("tp", None),
        P("tp", None),
        P("tp", None),
    )
    out_specs = (P("seq", "tp"), P("seq", None, "tp"))
    return jax.shard_map(shards, mesh=mesh, in_specs=in_specs, out_specs=out_specs, check_vma=False)
```

profile of v0, /device:TPU:0, one launch (start us, length us, event | category | flops | bytes accessed | tf_op | source)
XLA Modules:
  0.0 479.4 jit_solution(7024119431726332237)
XLA Ops:
  7.2 0.7 all-gather.5.cloned.1.call-update
  8.0 0.9 convert_reduce_fusion.1
  8.9 0.9 compare_and_fusion.1
  9.7 0.5 multiply_cosine_fusion
  10.3 20.2 %all-gather.5.cloned.1.call-done = bf16[256,2560]{1,0:T(8,128)(2,1)} async-done(((bf16[256,640]{1,0:T(8,128)(2,1)}), bf16[256,2560]{1,0:T(8,128)(2,1)}) %all-gather.5.cloned.1.call-update) | async-done | bytes 1310736 | tf_op jit(solution)/shard_map/all_gather | solution.py:83
  30.5 1.7 fusion.15
  32.2 3.9 fusion.56
  36.0 1.2 reshape.242
  37.2 2.5 fusion.58
  39.8 0.3 fusion.72
  40.1 0.3 fusion.88
  40.7 1.4 fusion.24
  42.1 1.9 convolution_convert_fusion.2
  44.1 2.0 convolution_convert_fusion.1
  46.0 2.4 copy.76
  48.5 26.6 %reduce-scatter.10.cloned.1.call-done = bf16[640,256]{1,0:T(8,128)(2,1)} async-done(((bf16[2560,256]{1,0:T(8,128)(2,1)}), bf16[640,256]{1,0:T(8,128)(2,1)}) %reduce-scatter.10.cloned.1.call-update) | async-done | bytes 327696
  75.2 1.2 copy.77
  76.4 0.8 fusion.49
  77.3 30.6 %all-gather = s32[2048,6]{0,1:T(8,128)S(1)} all-gather(s32[256,6]{0,1:T(8,128)S(1)} %copy-done.13), channel_id=2, replica_groups=mesh['seq'=8,'tp'=4] {'seq'}, dimensions={0}, use_global_device_ids=true | all-gather | bytes 55296 | tf_op jit(solution)/shard_map/all_gather | solution.py:141
  108.0 0.4 convert_reduce_fusion
  108.4 0.2 fusion.47
  108.6 0.4 bitcast_compare_fusion
  109.1 56.6 %all-gather.7.cloned.1.call-done = bf16[8192,640]{1,0:T(8,128)(2,1)} async-done(((bf16[256,640]{1,0:T(8,128)(2,1)}), bf16[8192,640]{1,0:T(8,128)(2,1)}) %all-gather.7.cloned.1.call-update) | async-done | bytes 10485776 | tf_op jit(solution)/shard_map/all_gather | solution.py:23
  165.7 6.1 %multiply_reduce_fusion = f32[8192]{0:T(1024)S(1)} fusion(bf16[8192,640]{1,0:T(8,128)(2,1)} %all-gather.7.cloned.1.call-done), kind=kLoop, calls=%fused_computation.1 | loop fusion | flops 15720448 | bytes 10518528 | tf_op jit(solution)/shard_map/reduce_sum | solution.py:33
  171.9 13.8 %copy.83 = f32[8,4,32,8,640]{4,3,1,2,0:T(8,128)} copy(bf16[8,4,32,8,640]{4,3,2,1,0:T(8,128)(2,1)} %bitcast.139) | data formatting | bytes 31457280 | tf_op jit(solution)/shard_map/convert_element_type | solution.py:133
  185.7 8.4 %multiply_convert_fusion = bf16[8,256,2560]{2,1,0:T(8,128)(2,1)S(1)} fusion(f32[8,256,2560]{2,1,0:T(8,128)} %bitcast.136, f32[2560]{0:T(1024)S(1)} %copy-done.12, f32[8,256]{1,0:T(8,128)S(1)} %add_rsqrt_fusion), kind=kLoop, calls=%fused_computation.3 | loop fusion | flops 15728640 | bytes 31475712 | tf_op jit(solution)/shard_map/convert_element_type | solution.py:133
  194.1 3.3 fusion.89
  197.3 0.6 copy-done.2
  198.0 0.5 select_reduce_fusion
  198.5 10.5 %convolution_convert_fusion = bf16[8,320,2560]{2,1,0:T(8,128)(2,1)} fusion(pred[8,320,256]{2,1,0:T(32,128)(4,1)S(1)} %bitcast_compare_fusion, bf16[8,256,2560]{2,1,0:T(8,128)(2,1)} %copy-done.2), kind=kOutput, calls=%fused_computation.13 | convolution fusion | flops 3361996800 | bytes 24248320 | tf_op jit(solution)/shard_map/wst,wtd->wsd/dot_general | solution.py:168
  209.1 14.1 %fusion.2 = f32[8,8,40,384]{3,2,1,0:T(8,128)} fusion(bf16[8,384,2560]{2,1,0:T(8,128)(2,1)} %param.29, bf16[8,8,40,2560]{3,2,1,0:T(8,128)(2,1)} %bitcast.140), kind=kOutput, calls=%fused_computation.6 | convolution fusion | flops 5033164800 | bytes 32768000 | tf_op jit(solution)/shard_map/secd,efd->secf/dot_general | solution.py:175
  223.1 24.0 %convert_bitcast_fusion = bf16[8,8,40,2560]{3,2,0,1:T(8,128)(2,1)} fusion(bf16[8,384,2560]{2,1,0:T(8,128)(2,1)} %param.30, f32[8,8,40,384]{3,2,1,0:T(8,128)} %fusion.2, bf16[8,384,2560]{2,1,0:T(8,128)(2,1)} %param.28, bf16[8,8,40,2560]{3,2,1,0:T(8,128)(2,1)} %bitcast.141, f32[8,8,40]{2,0,1:T(8,128)S(1)} %copy.67), kind=kOutput, calls=%fused_computation.10 | convolution fusion | flops 10079764480 | bytes 61614080 | tf_op jit(solution)/shard_map/secf,efd->secd/dot_general | solution.py:178
  247.2 12.5 %copy.68 = bf16[8,8,40,2560]{3,2,1,0:T(8,128)(2,1)} copy(bf16[8,8,40,2560]{3,2,0,1:T(8,128)(2,1)} %convert_bitcast_fusion) | data formatting | bytes 26214400 | tf_op jit(solution)/shard_map/convert_element_type | solution.py:179
  259.6 2.9 fusion.31
  262.6 4.3 fusion.43
  266.9 13.5 %add_convert_fusion = bf16[8,256,2560]{2,1,0:T(8,128)(2,1)} fusion(f32[256,2560]{1,0:T(8,128)S(1)} %fusion.43, pred[8]{0:T(512)(128)(4,1)S(1)} %iota_compare_fusion.5, pred[8,320,256]{2,1,0:T(32,128)(4,1)} %copy-done.4, bf16[8,320,2560]{2,1,0:T(8,128)(2,1)} %bitcast.142), kind=kOutput, calls=%fused_computation.2 | convolution fusion | flops 3371171840 | bytes 26869768 | tf_op jit(solution)/shard_map/wst,wsd->wtd/dot_general | solution.py:191
  280.4 14.7 %copy.78 = bf16[8,256,2560]{1,0,2:T(8,128)(2,1)} copy(bf16[8,256,2560]{2,1,0:T(8,128)(2,1)} %add_convert_fusion) | data formatting | bytes 20971520
  295.0 12.4 %copy.84 = bf16[320,8,8,256]{3,1,2,0:T(8,128)(2,1)} copy(bf16[320,8,8,256]{3,2,1,0:T(8,128)(2,1)} %bitcast.138) | data formatting | bytes 20971520
  307.5 83.9 %reduce-scatter.12.cloned.1.call-done = bf16[640,2048]{1,0:T(8,128)(2,1)} async-done(((bf16[2560,2048]{1,0:T(8,128)(2,1)}), bf16[640,2048]{1,0:T(8,128)(2,1)}) %reduce-scatter.12.cloned.1.call-update) | async-done | bytes 2621456
  391.4 4.1 copy.85
  395.6 5.0 %copy.79 = bf16[8,256,640]{2,1,0:T(8,128)(2,1)} copy(bf16[8,256,640]{1,0,2:T(8,128)(2,1)} %bitcast.143) | data formatting | bytes 5242880
  400.6 0.9 slice.42
  401.5 0.8 fusion.78
  402.3 0.7 pad_maximum_fusion
  403.0 1.7 copy.69
  404.6 1.7 scatter_fusion
  406.4 64.7 %reduce-scatter.8.cloned.1.call-done = bf16[1,256,640]{2,1,0:T(8,128)(2,1)} async-done(((bf16[8,256,640]{2,1,0:T(8,128)(2,1)}), bf16[1,256,640]{2,1,0:T(8,128)(2,1)}) %reduce-scatter.8.cloned.1.call-update) | async-done | bytes 327696 | tf_op jit(solution)/shard_map/reduce_scatter | solution.py:28
  471.1 1.8 fusion.48
  (54 shorter events, 0.8 us)
Async XLA Ops:
  7.2 36.9 %copy-start = (bf16[512,2560]{1,0:T(8,128)(2,1)S(1)}, bf16[512,2560]{1,0:T(8,128)(2,1)}, u32[]{:S(2)}) copy-start(bf16[512,2560]{1,0:T(8,128)(2,1)} %param.25) | copy-start | bytes 7864324
  7.2 23.3 %all-gather.5.cloned.1.call-start = ((), (), s32[]{:S(2)}) async-start(), calls=%async_computation.3 | async-start | bytes 1638400 | tf_op jit(solution)/shard_map/all_gather | solution.py:83
  7.9 67.3 %reduce-scatter.10.cloned.1.call-start = ((), (), s32[]{:S(2)}) async-start(), calls=%async_computation.6 | async-start | bytes 1638400
  10.3 27.0 %copy-start.14 = (f32[2560]{0:T(1024)S(1)}, f32[2560]{0:T(1024)}, u32[]{:S(2)}) copy-start(f32[2560]{0:T(1024)} %param.22) | copy-start | bytes 30724
  39.7 0.9 copy-start.11
  40.1 0.6 copy-start.9
  40.1 0.6 copy-start.10
  44.1 32.3 %copy-start.3 = (bf16[256,640]{1,0:T(8,128)(2,1)S(1)}, bf16[256,640]{1,0:T(8,128)(2,1)}, u32[]{:S(2)}) copy-start(bf16[256,640]{1,0:T(8,128)(2,1)} %param.17) | copy-start | bytes 983044
  46.0 31.3 %copy-start.13 = (s32[256,6]{0,1:T(8,128)S(1)}, s32[256,6]{0,1:T(8,128)}, u32[]{:S(2)}) copy-start(s32[256,6]{0,1:T(8,128)} %param.19) | copy-start | bytes 18436
  48.5 117.2 %all-gather.7.cloned.1.call-start = ((), (), s32[]{:S(2)}) async-start(), calls=%async_computation.5 | async-start | bytes 10813440 | tf_op jit(solution)/shard_map/all_gather | solution.py:23
  77.2 314.3 %reduce-scatter.12.cloned.1.call-start = ((), (), s32[]{:S(2)}) async-start(), calls=%async_computation.7 | async-start | bytes 13107200
  109.0 89.5 %copy-start.4 = (pred[8,320,256]{2,1,0:T(32,128)(4,1)}, pred[8,320,256]{2,1,0:T(32,128)(4,1)S(1)}, u32[]{:S(2)}) copy-start(pred[8,320,256]{2,1,0:T(32,128)(4,1)S(1)} %bitcast_compare_fusion) | copy-start | bytes 1966084
  171.9 13.8 %copy-start.12 = (f32[2560]{0:T(1024)S(1)}, f32[2560]{0:T(1024)}, u32[]{:S(2)}) copy-start(f32[2560]{0:T(1024)} %param.26) | copy-start | bytes 30724
  185.6 8.4 %copy-start.8 = (bf16[2560,64]{0,1:T(8,128)(2,1)S(1)}, bf16[2560,64]{0,1:T(8,128)(2,1)}, u32[]{:S(2)}) copy-start(bf16[2560,64]{0,1:T(8,128)(2,1)} %param.27) | copy-start | bytes 983044
  194.0 3.9 copy-start.2
  247.2 12.5 %copy-start.5 = (bf16[384,2560]{1,0:T(8,128)(2,1)S(1)}, bf16[384,2560]{1,0:T(8,128)(2,1)}, u32[]{:S(2)}) copy-start(bf16[384,2560]{1,0:T(8,128)(2,1)} %param.31) | copy-start | bytes 5898244
  307.5 163.6 %reduce-scatter.8.cloned.1.call-start = ((), (), s32[]{:S(2)}) async-start(), calls=%async_computation.4 | async-start | bytes 2949120 | tf_op jit(solution)/shard_map/reduce_scatter | solution.py:28
  395.6 77.3 %copy-start.1 = (bf16[512,2560]{1,0:T(8,128)(2,1)S(1)}, bf16[512,2560]{1,0:T(8,128)(2,1)}, u32[]{:S(2)}) copy-start(bf16[512,2560]{1,0:T(8,128)(2,1)} %param.25) | copy-start | bytes 7864324
  395.6 5.0 %copy-start.15 = (s32[1,32]{1,0:T(1,128)S(1)}, s32[1,32]{1,0:T(1,128)}, u32[]{:S(2)}) copy-start(s32[1,32]{1,0:T(1,128)} %param.20) | copy-start | bytes 388
  395.6 9.1 %copy-start.7 = (bf16[32,16,256]{2,1,0:T(8,128)(2,1)S(1)}, bf16[32,16,256]{2,1,0:T(8,128)(2,1)}, u32[]{:S(2)}) copy-start(bf16[32,16,256]{2,1,0:T(8,128)(2,1)} %param.21) | copy-start | bytes 786436
  406.3 66.6 %copy-start.6 = (bf16[32,16,256]{2,1,0:T(8,128)(2,1)}, bf16[32,16,256]{2,1,0:T(8,128)(2,1)S(1)}, u32[]{:S(2)}) copy-start(bf16[32,16,256]{2,1,0:T(8,128)(2,1)S(1)} %scatter_fusion) | copy-start | bytes 786436
Sparse Core Ops, SparseCore 0:
  9.6 20.8 all-gather.4
  48.6 26.5 reduce-scatter.9
  79.0 86.6 all-gather.6
  307.6 83.8 reduce-scatter.11
  400.7 70.3 reduce-scatter.7
where the time goes:
time: 481 us; the launch traced here: 479 us
  waiting for transfers between devices  253 us (53%)
  matrix products  84.5 us (18%)
  local copies, waits for them, and re-layouts  72.8 us (15%)
  blocking collectives  30.6 us (6%)
  other arithmetic  24.3 us (5%)
  between operations  14.1 us (3%)
    unnamed x7, waiting for transfers between devices  111 us
    reduce_scatter x1, waiting for transfers between devices, scatter_all(): return lax.psum_scatter(part, 'seq', scatter_dimension=0, tiled=False)  64.7 us
    all_gather x1, waiting for transfers between devices, gather_all(): return lax.all_gather(block, ('seq', 'tp'), axis=0)  56.6 us
    unnamed x38, local copies, waits for them, and re-layouts  40.6 us
    all_gather x1, blocking collectives, shards(): routes_all = lax.all_gather(routes, 'seq', axis=0)  30.6 us
    dot_general x1, matrix products, shards(): jnp.einsum('secf,efd->secd', activation, expert_down, preferred_element_t...  24 us
    all_gather x1, waiting for transfers between devices, shards(): whole_rows = lax.all_gather(tokens, 'tp', axis=1, tiled=True)  20.2 us
    dot_general x1, matrix products, shards(): jnp.einsum('secd,efd->secf', slot_rows, expert_up, preferred_element_type...  14.1 us
  transfers between devices with their start and end apart: 5, of which 5 were waited for; matrix products, arithmetic and copies ran while one was open for 2% of the time, Pallas kernels for 0%

commit v1 on v0

--- a/solution.py
+++ b/solution.py
@@ -7,6 +7,19 @@
 PAGE = 16
 norm_eps = 1e-05
 rope_base = 500000.0
+
+
+def gather_around(shard, axis, dim):
+    peers, index, width = (lax.axis_size(axis), lax.axis_index(axis), shard.shape[dim])
+    right = [(i, (i + 1) % peers) for i in range(peers)]
+    out = jnp.zeros((*shard.shape[:dim], peers * width, *shard.shape[dim + 1 :]), shard.dtype)
+    current = shard
+    for step in range(peers):
+        source = (index - step) % peers
+        out = lax.dynamic_update_slice_in_dim(out, current, source * width, axis=dim)
+        if step < peers - 1:
+            current = lax.ppermute(current, axis, right)
+    return out
 
 
 def partner(block, axis, distance):
@@ -80,7 +93,7 @@
     row_count = tokens.shape[0]
     col_width = tokens.shape[1]
     model_width = col_width * tp_count
-    whole_rows = lax.all_gather(tokens, "tp", axis=1, tiled=True)
+    whole_rows = gather_around(tokens, "tp", 1)
     residual = whole_rows.astype(jnp.float32)
     normed_in = rms_scale(residual, attn_gain).astype(jnp.bfloat16)
     segment_row = segments[0]

time: 481 us -> 477 us (level)
    all_gather x1 -> x0, waiting for transfers between devices: 20.2 us -> none  [shards(): whole_rows = lax.all_gather(tokens, 'tp', axis=1, tiled=True)]
    ppermute x0 -> x3, waiting for transfers between devices: none -> 16.3 us  [gather_around(): current = lax.ppermute(current, axis, right)]
    unnamed x7 -> x6, waiting for transfers between devices: 111 us -> 113 us
    unnamed x38 -> x42, local copies, waits for them, and re-layouts: 40.6 us -> 40.7 us
  transfers between devices with their start and end apart: 5 -> 7, of which waited for: 5 -> 7; matrix products, arithmetic and copies ran while one was open for 2% -> 2% of each run, Pallas kernels for 0% -> 0%
where the time goes in v1:
time: 477 us; the launch traced here: 475 us
  waiting for transfers between devices  251 us (53%)
  matrix products  81.3 us (17%)
  local copies, waits for them, and re-layouts  75 us (16%)
  blocking collectives  30.6 us (6%)
  other arithmetic  23.1 us (5%)
  between operations  14.1 us (3%)
    unnamed x6, waiting for transfers between devices  113 us
    reduce_scatter x1, waiting for transfers between devices, scatter_all(): return lax.psum_scatter(part, 'seq', scatter_dimension=0, tiled=False)  65 us
    all_gather x1, waiting for transfers between devices, gather_all(): return lax.all_gather(block, ('seq', 'tp'), axis=0)  56.6 us
    unnamed x42, local copies, waits for them, and re-layouts  40.7 us
    all_gather x1, blocking collectives, shards(): routes_all = lax.all_gather(routes, 'seq', axis=0)  30.6 us
    dot_general x1, matrix products, shards(): jnp.einsum('secf,efd->secd', activation, expert_down, preferred_element_t...  24 us
    ppermute x3, waiting for transfers between devices, gather_around(): current = lax.ppermute(current, axis, right)  16.3 us
    dot_general x1, matrix products, shards(): jnp.einsum('secd,efd->secf', slot_rows, expert_up, preferred_element_type...  14.1 us
  transfers between devices with their start and end apart: 7, of which 7 were waited for; matrix products, arithmetic and copies ran while one was open for 2% of the time, Pallas kernels for 0%

profile of v1, /device:TPU:0, one launch (start us, length us, event | category | flops | bytes accessed | tf_op | source)
XLA Modules:
  0.0 475.4 jit_solution(14007602383540801382)
XLA Ops:
  7.2 0.5 collective-permute-start
  7.7 0.9 convert_reduce_fusion.1
  8.7 0.9 compare_and_fusion.1
  9.6 5.1 %collective-permute-done = bf16[256,640]{1,0:T(8,128)(2,1)S(1)} collective-permute-done((bf16[256,640]{1,0:T(8,128)(2,1)}, bf16[256,640]{1,0:T(8,128)(2,1)S(1)}, u32[]{:S(2)}, u32[]{:S(2)}) %collective-permute-start) | collective-permute-done | bytes 327712 | tf_op jit(solution)/shard_map/ppermute | solution.py:21
  14.7 0.5 multiply_cosine_fusion
  15.2 5.9 %collective-permute-done.1 = bf16[256,640]{1,0:T(8,128)(2,1)S(1)} collective-permute-done((bf16[256,640]{1,0:T(8,128)(2,1)S(1)}, bf16[256,640]{1,0:T(8,128)(2,1)S(1)}, u32[]{:S(2)}, u32[]{:S(2)}) %collective-permute-start.1) | collective-permute-done | bytes 327712 | tf_op jit(solution)/shard_map/ppermute | solution.py:21
  21.2 1.0 constant_dynamic-update-slice_fusion.3
  22.4 5.3 %collective-permute-done.2 = bf16[256,640]{1,0:T(8,128)(2,1)S(1)} collective-permute-done((bf16[256,640]{1,0:T(8,128)(2,1)S(1)}, bf16[256,640]{1,0:T(8,128)(2,1)S(1)}, u32[]{:S(2)}, u32[]{:S(2)}) %collective-permute-start.2) | collective-permute-done | bytes 327712 | tf_op jit(solution)/shard_map/ppermute | solution.py:21
  28.0 1.5 fusion.58
  29.6 1.7 fusion.56
  31.2 1.2 reshape.242
  32.5 0.9 slice_bitcast_fusion
  34.3 1.4 fusion.24
  35.7 1.9 convolution_convert_fusion.2
  37.6 1.9 convolution_convert_fusion.1
  39.6 2.5 copy.76
  42.1 28.7 %reduce-scatter.10.cloned.1.call-done = bf16[640,256]{1,0:T(8,128)(2,1)} async-done(((bf16[2560,256]{1,0:T(8,128)(2,1)}), bf16[640,256]{1,0:T(8,128)(2,1)}) %reduce-scatter.10.cloned.1.call-update) | async-done | bytes 327696
  70.8 1.2 copy.77
  72.0 0.8 fusion.49
  73.0 30.6 %all-gather = s32[2048,6]{0,1:T(8,128)S(1)} all-gather(s32[256,6]{0,1:T(8,128)S(1)} %copy-done.13), channel_id=2, replica_groups=mesh['seq'=8,'tp'=4] {'seq'}, dimensions={0}, use_global_device_ids=true | all-gather | bytes 55296 | tf_op jit(solution)/shard_map/all_gather | solution.py:154
  103.6 0.4 convert_reduce_fusion
  104.2 0.4 bitcast_compare_fusion
  104.7 56.6 %all-gather.4.cloned.1.call-done = bf16[8192,640]{1,0:T(8,128)(2,1)} async-done(((bf16[256,640]{1,0:T(8,128)(2,1)}), bf16[8192,640]{1,0:T(8,128)(2,1)}) %all-gather.4.cloned.1.call-update) | async-done | bytes 10485776 | tf_op jit(solution)/shard_map/all_gather | solution.py:36
  161.3 6.1 %multiply_reduce_fusion = f32[8192]{0:T(1024)S(1)} fusion(bf16[8192,640]{1,0:T(8,128)(2,1)} %all-gather.4.cloned.1.call-done), kind=kLoop, calls=%fused_computation.1 | loop fusion | flops 15720448 | bytes 10518528 | tf_op jit(solution)/shard_map/reduce_sum | solution.py:46
  167.5 13.8 %copy.83 = f32[8,4,32,8,640]{4,3,1,2,0:T(8,128)} copy(bf16[8,4,32,8,640]{4,3,2,1,0:T(8,128)(2,1)} %bitcast.139) | data formatting | bytes 31457280 | tf_op jit(solution)/shard_map/convert_element_type | solution.py:146
  181.3 8.4 %multiply_convert_fusion = bf16[8,256,2560]{2,1,0:T(8,128)(2,1)S(1)} fusion(f32[8,256,2560]{2,1,0:T(8,128)} %bitcast.136, f32[2560]{0:T(1024)S(1)} %copy-done.12, f32[8,256]{1,0:T(8,128)S(1)} %add_rsqrt_fusion), kind=kLoop, calls=%fused_computation.3 | loop fusion | flops 15728640 | bytes 31475712 | tf_op jit(solution)/shard_map/convert_element_type | solution.py:146
  189.7 3.3 fusion.89
  193.0 0.6 copy-done.2
  193.6 0.5 select_reduce_fusion
  194.1 10.5 %convolution_convert_fusion = bf16[8,320,2560]{2,1,0:T(8,128)(2,1)} fusion(pred[8,320,256]{2,1,0:T(32,128)(4,1)S(1)} %bitcast_compare_fusion, bf16[8,256,2560]{2,1,0:T(8,128)(2,1)} %copy-done.2), kind=kOutput, calls=%fused_computation.13 | convolution fusion | flops 3361996800 | bytes 24248320 | tf_op jit(solution)/shard_map/wst,wtd->wsd/dot_general | solution.py:181
  204.7 14.1 %fusion.2 = f32[8,8,40,384]{3,2,1,0:T(8,128)} fusion(bf16[8,384,2560]{2,1,0:T(8,128)(2,1)} %param.29, bf16[8,8,40,2560]{3,2,1,0:T(8,128)(2,1)} %bitcast.140), kind=kOutput, calls=%fused_computation.6 | convolution fusion | flops 5033164800 | bytes 32768000 | tf_op jit(solution)/shard_map/secd,efd->secf/dot_general | solution.py:188
  218.8 24.0 %convert_bitcast_fusion = bf16[8,8,40,2560]{3,2,0,1:T(8,128)(2,1)} fusion(bf16[8,384,2560]{2,1,0:T(8,128)(2,1)} %param.30, f32[8,8,40,384]{3,2,1,0:T(8,128)} %fusion.2, bf16[8,384,2560]{2,1,0:T(8,128)(2,1)} %param.28, bf16[8,8,40,2560]{3,2,1,0:T(8,128)(2,1)} %bitcast.141, f32[8,8,40]{2,0,1:T(8,128)S(1)} %copy.67), kind=kOutput, calls=%fused_computation.10 | convolution fusion | flops 10079764480 | bytes 61614080 | tf_op jit(solution)/shard_map/secf,efd->secd/dot_general | solution.py:191
  242.8 12.5 %copy.68 = bf16[8,8,40,2560]{3,2,1,0:T(8,128)(2,1)} copy(bf16[8,8,40,2560]{3,2,0,1:T(8,128)(2,1)} %convert_bitcast_fusion) | data formatting | bytes 26214400 | tf_op jit(solution)/shard_map/convert_element_type | solution.py:192
  255.3 2.9 fusion.31
  258.2 4.3 fusion.43
  262.5 13.5 %add_convert_fusion = bf16[8,256,2560]{2,1,0:T(8,128)(2,1)} fusion(f32[256,2560]{1,0:T(8,128)S(1)} %fusion.43, pred[8]{0:T(512)(128)(4,1)S(1)} %iota_compare_fusion.5, pred[8,320,256]{2,1,0:T(32,128)(4,1)} %copy-done.4, bf16[8,320,2560]{2,1,0:T(8,128)(2,1)} %bitcast.142), kind=kOutput, calls=%fused_computation.2 | convolution fusion | flops 3371171840 | bytes 26869768 | tf_op jit(solution)/shard_map/wst,wsd->wtd/dot_general | solution.py:204
  276.0 14.7 %copy.78 = bf16[8,256,2560]{1,0,2:T(8,128)(2,1)} copy(bf16[8,256,2560]{2,1,0:T(8,128)(2,1)} %add_convert_fusion) | data formatting | bytes 20971520
  290.7 12.4 %copy.84 = bf16[320,8,8,256]{3,1,2,0:T(8,128)(2,1)} copy(bf16[320,8,8,256]{3,2,1,0:T(8,128)(2,1)} %bitcast.138) | data formatting | bytes 20971520
  303.2 83.9 %reduce-scatter.12.cloned.1.call-done = bf16[640,2048]{1,0:T(8,128)(2,1)} async-done(((bf16[2560,2048]{1,0:T(8,128)(2,1)}), bf16[640,2048]{1,0:T(8,128)(2,1)}) %reduce-scatter.12.cloned.1.call-update) | async-done | bytes 2621456
  387.1 4.1 copy.85
  391.2 5.0 %copy.79 = bf16[8,256,640]{2,1,0:T(8,128)(2,1)} copy(bf16[8,256,640]{1,0,2:T(8,128)(2,1)} %bitcast.143) | data formatting | bytes 5242880
  396.3 0.9 slice.42
  397.2 0.8 fusion.78
  398.0 0.7 pad_maximum_fusion
  398.6 1.7 copy.69
  400.3 1.7 scatter_fusion
  402.0 65.0 %reduce-scatter.8.cloned.1.call-done = bf16[1,256,640]{2,1,0:T(8,128)(2,1)} async-done(((bf16[8,256,640]{2,1,0:T(8,128)(2,1)}), bf16[1,256,640]{2,1,0:T(8,128)(2,1)}) %reduce-scatter.8.cloned.1.call-update) | async-done | bytes 327696 | tf_op jit(solution)/shard_map/reduce_scatter | solution.py:41
  467.0 1.8 fusion.48
  (66 shorter events, 2.2 us)
Async XLA Ops:
  7.2 30.5 %copy-start = (bf16[512,2560]{1,0:T(8,128)(2,1)S(1)}, bf16[512,2560]{1,0:T(8,128)(2,1)}, u32[]{:S(2)}) copy-start(bf16[512,2560]{1,0:T(8,128)(2,1)} %param.25) | copy-start | bytes 7864324
  7.2 20.9 %copy-start.16 = (f32[2560]{0:T(1024)S(1)}, f32[2560]{0:T(1024)}, u32[]{:S(2)}) copy-start(f32[2560]{0:T(1024)} %param.22) | copy-start | bytes 30724
  7.2 63.6 %reduce-scatter.10.cloned.1.call-start = ((), (), s32[]{:S(2)}) async-start(), calls=%async_computation.5 | async-start | bytes 1638400
  7.2 7.4 %collective-permute-start = (bf16[256,640]{1,0:T(8,128)(2,1)}, bf16[256,640]{1,0:T(8,128)(2,1)S(1)}, u32[]{:S(2)}, u32[]{:S(2)}) collective-permute-start(bf16[256,640]{1,0:T(8,128)(2,1)} %param.17), channel_id=1, source_target_pairs={{0,1},{1,2},{2,3},{3,0},{4,5},{5,6},{6,7},{7,4},{8,9},{9,10},{10,1... | collective-permute-start | bytes 983048 | tf_op jit(solution)/shard_map/ppermute | solution.py:21
  8.6 19.4 %copy-start.15 = (bf16[2560,256]{1,0:T(8,128)(2,1)S(1)}, bf16[2560,256]{1,0:T(8,128)(2,1)}, u32[]{:S(2)}) copy-start(bf16[2560,256]{1,0:T(8,128)(2,1)} %param.24) | copy-start | bytes 3932164
  14.6 6.5 %collective-permute-start.1 = (bf16[256,640]{1,0:T(8,128)(2,1)S(1)}, bf16[256,640]{1,0:T(8,128)(2,1)S(1)}, u32[]{:S(2)}, u32[]{:S(2)}) collective-permute-start(bf16[256,640]{1,0:T(8,128)(2,1)S(1)} %collective-permute-done), channel_id=1, source_target_pairs={{0,1},{1,2},{2,3},{3,0},{4,5},{5,6},{6,7},{7,4},{8,9},{9,10},{10,1... | collective-permute-start | bytes 983048 | tf_op jit(solution)/shard_map/ppermute | solution.py:21
  21.1 6.5 %collective-permute-start.2 = (bf16[256,640]{1,0:T(8,128)(2,1)S(1)}, bf16[256,640]{1,0:T(8,128)(2,1)S(1)}, u32[]{:S(2)}, u32[]{:S(2)}) collective-permute-start(bf16[256,640]{1,0:T(8,128)(2,1)S(1)} %collective-permute-done.1), channel_id=1, source_target_pairs={{0,1},{1,2},{2,3},{3,0},{4,5},{5,6},{6,7},{7,4},{8,9},{9,10},{10,1... | collective-permute-start | bytes 983048 | tf_op jit(solution)/shard_map/ppermute | solution.py:21
  22.3 7.2 %copy-start.14 = (bf16[2560,512]{1,0:T(8,128)(2,1)S(1)}, bf16[2560,512]{1,0:T(8,128)(2,1)}, u32[]{:S(2)}) copy-start(bf16[2560,512]{1,0:T(8,128)(2,1)} %param.23) | copy-start | bytes 7864324
  33.7 0.6 copy-start.9
  33.7 0.6 copy-start.10
  34.1 1.7 copy-start.11
  39.6 32.4 %copy-start.3 = (bf16[256,640]{1,0:T(8,128)(2,1)S(1)}, bf16[256,640]{1,0:T(8,128)(2,1)}, u32[]{:S(2)}) copy-start(bf16[256,640]{1,0:T(8,128)(2,1)} %param.17) | copy-start | bytes 983044
  39.6 33.4 %copy-start.13 = (s32[256,6]{0,1:T(8,128)S(1)}, s32[256,6]{0,1:T(8,128)}, u32[]{:S(2)}) copy-start(s32[256,6]{0,1:T(8,128)} %param.19) | copy-start | bytes 18436
  42.1 119.2 %all-gather.4.cloned.1.call-start = ((), (), s32[]{:S(2)}) async-start(), calls=%async_computation.4 | async-start | bytes 10813440 | tf_op jit(solution)/shard_map/all_gather | solution.py:36
  72.8 314.2 %reduce-scatter.12.cloned.1.call-start = ((), (), s32[]{:S(2)}) async-start(), calls=%async_computation.6 | async-start | bytes 13107200
  104.7 89.5 %copy-start.4 = (pred[8,320,256]{2,1,0:T(32,128)(4,1)}, pred[8,320,256]{2,1,0:T(32,128)(4,1)S(1)}, u32[]{:S(2)}) copy-start(pred[8,320,256]{2,1,0:T(32,128)(4,1)S(1)} %bitcast_compare_fusion) | copy-start | bytes 1966084
  167.5 13.8 %copy-start.12 = (f32[2560]{0:T(1024)S(1)}, f32[2560]{0:T(1024)}, u32[]{:S(2)}) copy-start(f32[2560]{0:T(1024)} %param.26) | copy-start | bytes 30724
  181.3 8.4 %copy-start.8 = (bf16[2560,64]{0,1:T(8,128)(2,1)S(1)}, bf16[2560,64]{0,1:T(8,128)(2,1)}, u32[]{:S(2)}) copy-start(bf16[2560,64]{0,1:T(8,128)(2,1)} %param.27) | copy-start | bytes 983044
  189.7 3.9 copy-start.2
  242.8 12.5 %copy-start.5 = (bf16[384,2560]{1,0:T(8,128)(2,1)S(1)}, bf16[384,2560]{1,0:T(8,128)(2,1)}, u32[]{:S(2)}) copy-start(bf16[384,2560]{1,0:T(8,128)(2,1)} %param.31) | copy-start | bytes 5898244
  303.1 163.9 %reduce-scatter.8.cloned.1.call-start = ((), (), s32[]{:S(2)}) async-start(), calls=%async_computation.3 | async-start | bytes 2949120 | tf_op jit(solution)/shard_map/reduce_scatter | solution.py:41
  391.2 5.0 %copy-start.17 = (s32[1,32]{1,0:T(1,128)S(1)}, s32[1,32]{1,0:T(1,128)}, u32[]{:S(2)}) copy-start(s32[1,32]{1,0:T(1,128)} %param.20) | copy-start | bytes 388
  391.2 9.1 %copy-start.7 = (bf16[32,16,256]{2,1,0:T(8,128)(2,1)S(1)}, bf16[32,16,256]{2,1,0:T(8,128)(2,1)}, u32[]{:S(2)}) copy-start(bf16[32,16,256]{2,1,0:T(8,128)(2,1)} %param.21) | copy-start | bytes 786436
  391.2 77.6 %copy-start.1 = (bf16[512,2560]{1,0:T(8,128)(2,1)S(1)}, bf16[512,2560]{1,0:T(8,128)(2,1)}, u32[]{:S(2)}) copy-start(bf16[512,2560]{1,0:T(8,128)(2,1)} %param.25) | copy-start | bytes 7864324
  402.0 66.8 %copy-start.6 = (bf16[32,16,256]{2,1,0:T(8,128)(2,1)}, bf16[32,16,256]{2,1,0:T(8,128)(2,1)S(1)}, u32[]{:S(2)}) copy-start(bf16[32,16,256]{2,1,0:T(8,128)(2,1)S(1)} %scatter_fusion) | copy-start | bytes 786436
Sparse Core Ops, SparseCore 0:
  42.2 28.5 reduce-scatter.9
  74.6 86.6 all-gather.3
  303.2 83.7 reduce-scatter.11
  396.4 70.5 reduce-scatter.7
